TPU v7x, 256 devices: a whole 4x4x8 slice. The times are simulated.
256 devices in a mesh: src: 64 (over z_hi, x, y, core), rcv: 4 (over z_lo).
Axes of the slice: x: 4, y: 4, z: 8 (z_hi: 2, z_lo: 4; z = z_hi * 4 + z_lo), core: 2. Of those that a mesh axis runs over, the one named last changes fastest.
Arguments:
- src_spec: bfloat16 [2, 16, 256, 4096], P(None, None, 'rcv', 'src'), may hold values from -6 to 6
- rcv_spec: bfloat16 [2, 16, 256, 1024], P(None, None, 'src', 'rcv'), may hold values from -6 to 6
- lag_table: int32 [16, 8192], replicated, may hold values from 0 to 511
- src_pos: int32 [4096], P('src'), may hold values from 0 to 8191
- rcv_pos: int32 [1024], P('rcv'), may hold values from 0 to 8191
Outputs:
- panel_src: float32 [16, 2, 4096, 256], P(None, None, ('src', 'rcv'))
- panel_rcv: float32 [16, 2, 256, 1024], P(None, None, 'src', 'rcv')
All inputs are finite; a program needn't handle non-finite values.
Results may differ from a plain program's by a relative error of at most 0.0035.
Values may be sent and summed in bfloat16 or wider, within the bound.
A program may use at most 64 MiB of HBM per device.

v0:
```python
import math
import jax
import jax.numpy as jnp
from jax import lax
from jax.sharding import PartitionSpec as P

WIN = 8
SEGS = 2


def phase_table(freqs, lags, n_freq):
    index_mod = freqs[:, None, None] * jnp.transpose(lags)[None, :, :] % (2 * n_freq)
    angles = index_mod.astype(jnp.float32) * (math.pi / n_freq)
    return (jnp.cos(angles), jnp.sin(angles))


def cross_block(src_block, rcv_block):
    block_width = src_block.shape[2]
    src_five = src_block.reshape(2, SEGS, WIN, block_width, src_block.shape[3])
    rcv_five = rcv_block.reshape(2, SEGS, WIN, block_width, rcv_block.shape[3])
    swapped = jnp.stack([src_five[1], -src_five[0]])
    real_part = jnp.einsum(
        "cgwfs,cgwfr->gfsr", src_five, rcv_five, preferred_element_type=jnp.float32
    )
    imag_part = jnp.einsum(
        "cgwfs,cgwfr->gfsr", swapped, rcv_five, preferred_element_type=jnp.float32
    )
    floor_mod = jnp.maximum(jnp.sqrt(real_part * real_part + imag_part * imag_part), 1.0)
    stacked_re = (jnp.sum(real_part / floor_mod, axis=0) / SEGS).astype(jnp.bfloat16)
    stacked_im = (jnp.sum(imag_part / floor_mod, axis=0) / SEGS).astype(jnp.bfloat16)
    return (stacked_re, stacked_im)


def source_slant(stacked_re, stacked_im, rcv_cos, rcv_sin, src_cos, src_sin, factor):
    left_op = jnp.concatenate([stacked_re, stacked_im], axis=2)
    cos_b = rcv_cos.astype(jnp.bfloat16)
    sin_b = rcv_sin.astype(jnp.bfloat16)
    upper_half = jnp.concatenate([cos_b, sin_b], axis=2)
    bottom = jnp.concatenate([-sin_b, cos_b], axis=2)
    right_op = jnp.concatenate([upper_half, bottom], axis=1)
    sums = jnp.einsum("fsk,fkq->fsq", left_op, right_op, preferred_element_type=jnp.float32)
    n_slow = rcv_cos.shape[2]
    sum_re = sums[:, :, :n_slow]
    sum_im = sums[:, :, n_slow:]
    panel_re = (sum_re * src_cos + sum_im * src_sin) * factor
    panel_im = (sum_im * src_cos - sum_re * src_sin) * factor
    return jnp.transpose(jnp.stack([panel_re, panel_im]), (3, 0, 2, 1))


def receiver_right(src_cos_b, src_sin_b):
    upper_half = jnp.concatenate([src_cos_b, -src_sin_b], axis=2)
    bottom = jnp.concatenate([src_sin_b, src_cos_b], axis=2)
    return jnp.concatenate([upper_half, bottom], axis=1)


def receiver_sums(left_op, right_op):
    return jnp.einsum("fkr,fkq->fqr", left_op, right_op, preferred_element_type=jnp.float32)


def receiver_outer(sums, rcv_cos, rcv_sin, factor):
    n_slow = rcv_cos.shape[2]
    cos_t = jnp.transpose(rcv_cos, (0, 2, 1))
    sin_t = jnp.transpose(rcv_sin, (0, 2, 1))
    sum_re = sums[:, :n_slow, :]
    sum_im = sums[:, n_slow:, :]
    panel_re = (sum_re * cos_t - sum_im * sin_t) * factor
    panel_im = (sum_re * sin_t + sum_im * cos_t) * factor
    return jnp.transpose(jnp.stack([panel_re, panel_im]), (2, 0, 1, 3))


def per_device(src_spec, rcv_spec, lag_table, src_pos, rcv_pos):
    src_full = lax.all_gather(src_spec, "rcv", axis=2, tiled=True)
    n_freq = src_full.shape[2]
    src_dev = src_full.shape[3]
    rcv_dev = rcv_spec.shape[3]
    n_slow = lag_table.shape[0]
    n_src = lax.axis_size("src")
    n_rcv = lax.axis_size("rcv")
    src_factor = 1.0 / math.sqrt(rcv_dev * n_rcv)
    rcv_factor = 1.0 / math.sqrt(src_dev * n_src)
    lag_src = jnp.take(lag_table, src_pos, axis=1)
    lag_rcv = jnp.take(lag_table, rcv_pos, axis=1)
    src_init = jnp.zeros((n_slow, 2, src_dev, n_freq), jnp.float32)
    other_init = jnp.zeros((n_slow, 2, n_freq, rcv_dev), jnp.float32)
    shard_piece = lax.all_gather(rcv_spec, "src", axis=2, tiled=True)
    block_width = math.gcd(shard_piece.shape[2], 16)

    def inner(turn_index, totals):
        offset = turn_index * block_width
        freqs = offset + jnp.arange(block_width, dtype=jnp.int32)
        src_block = lax.dynamic_slice_in_dim(src_full, offset, block_width, 2)
        rcv_block = lax.dynamic_slice_in_dim(shard_piece, offset, block_width, 2)
        stacked_re, stacked_im = cross_block(src_block, rcv_block)
        rcv_cos, rcv_sin = phase_table(freqs, lag_rcv, n_freq)
        src_cos, src_sin = phase_table(freqs, lag_src, n_freq)
        src_part = source_slant(
            stacked_re, stacked_im, rcv_cos, rcv_sin, src_cos, src_sin, src_factor
        )
        src_total = lax.dynamic_update_slice_in_dim(totals[0], src_part, offset, 3)
        left_op = jnp.concatenate([stacked_re, stacked_im], axis=1)
        right_op = receiver_right(src_cos.astype(jnp.bfloat16), src_sin.astype(jnp.bfloat16))
        rcv_part = receiver_outer(receiver_sums(left_op, right_op), rcv_cos, rcv_sin, rcv_factor)
        other = lax.dynamic_update_slice_in_dim(totals[1], rcv_part, offset, 2)
        return (src_total, other)

    src_total, other = lax.fori_loop(
        0, shard_piece.shape[2] // block_width, inner, (src_init, other_init)
    )
    panel_src = lax.psum_scatter(src_total, "rcv", scatter_dimension=2, tiled=True)
    panel_rcv = lax.psum_scatter(other, "src", scatter_dimension=2, tiled=True)
    return (panel_src, panel_rcv)


def solution(mesh):
    placed = (P(None, None, "rcv", "src"), P(None, None, "src", "rcv"), P(), P("src"), P("rcv"))
    return jax.shard_map(
        per_device,
        mesh=mesh,
        in_specs=placed,
        out_specs=(P(None, None, ("src", "rcv"), None), P(None, None, "src", "rcv")),
        check_vma=False,
    )
```

profile of v0, /device:TPU:1, one launch (start us, length us, event | category | flops | bytes accessed | tf_op | source)
XLA Modules:
  0.0 853.7 jit_solution(8564354730002031349)
XLA Ops:
  8.0 1.5 copy.29
  9.5 3.5 copy.30
  13.0 2.8 gather_fusion.1
  15.9 2.9 gather_fusion
  19.1 44.0 %all-gather.3.cloned.1.call-done = bf16[2,16,256,64]{3,2,1,0:T(8,128)(2,1)} async-done(((bf16[2,16,64,64]{3,2,1,0:T(8,128)(2,1)}), bf16[2,16,256,64]{3,2,1,0:T(8,128)(2,1)}) %all-gather.3.cloned.1.call-update) | async-done | bytes 1048592 | tf_op jit(solution)/shard_map/all_gather | solution.py:72
  63.1 97.3 %all-gather.5.cloned.1.call-done = bf16[2,16,256,256]{3,1,0,2:T(8,128)(2,1)} async-done(((bf16[2,16,4,256]{3,1,0,2:T(8,128)(2,1)}), bf16[2,16,256,256]{3,1,0,2:T(8,128)(2,1)}) %all-gather.5.cloned.1.call-update) | async-done | bytes 4194320 | tf_op jit(solution)/shard_map/all_gather | solution.py:85
  160.4 2.2 broadcast_in_dim.40
  162.6 4.3 broadcast_in_dim.41.clone
  166.9 212.6 %while.17 = (s32[]{:T(128)}, f32[16,2,64,256]{2,0,3,1:T(8,128)}, f32[16,2,256,256]{3,0,1,2:T(8,128)}, bf16[2,16,256,64]{3,2,1,0:T(8,128)(2,1)}, bf16[2,16,256,25...) while((s32[]{:T(128)}, f32[16,2,64,256]{2,0,3,1:T(8,128)}, ...), condition=%wide.region_3.4_spmd, body=%wide.region_0.3_spmd.sunk | while | flops 116801552 | bytes 17031760 | solution.py:106
  171.7 1.4 fusion.76
  173.2 2.5 fusion.77
  177.4 1.3 multiply_bitcast_fusion.5
  185.0 1.4 fusion.76
  186.5 2.5 fusion.77
  190.7 1.3 multiply_bitcast_fusion.5
  198.3 1.4 fusion.76
  199.8 2.5 fusion.77
  211.6 1.4 fusion.76
  213.1 2.5 fusion.77
  217.2 1.3 multiply_bitcast_fusion.5
  224.9 1.4 fusion.76
  226.4 2.5 fusion.77
  238.2 1.4 fusion.76
  239.6 2.5 fusion.77
  251.5 1.4 fusion.76
  252.9 2.5 fusion.77
  264.8 1.4 fusion.76
  266.2 2.5 fusion.77
  278.1 1.4 fusion.76
  279.5 2.5 fusion.77
  291.4 1.4 fusion.76
  292.8 2.5 fusion.77
  304.6 1.4 fusion.76
  306.1 2.5 fusion.77
  317.9 1.4 fusion.76
  319.4 2.5 fusion.77
  331.2 1.4 fusion.76
  332.6 2.5 fusion.77
  344.5 1.4 fusion.76
  345.9 2.5 fusion.77
  357.8 1.4 fusion.76
  359.2 2.5 fusion.77
  371.1 1.4 fusion.76
  372.5 2.5 fusion.77
  379.6 3.8 copy.35
  383.5 410.5 %reduce-scatter.5.cloned.1.call-done = f32[16,2,4,256]{3,0,1,2:T(8,128)} async-done(((f32[16,2,256,256]{3,0,1,2:T(8,128)}), f32[16,2,4,256]{3,0,1,2:T(8,128)}) %reduce-scatter.5.cloned.1.call-update) | async-done | bytes 131088 | tf_op jit(solution)/shard_map/reduce_scatter | solution.py:110
  794.0 1.6 copy.37
  795.6 51.6 %reduce-scatter.3.cloned.1.call-done = f32[16,2,16,256]{3,2,1,0:T(8,128)} async-done(((f32[16,2,64,256]{3,2,1,0:T(8,128)}), f32[16,2,16,256]{3,2,1,0:T(8,128)}) %reduce-scatter.3.cloned.1.call-update) | async-done | bytes 524304 | tf_op jit(solution)/shard_map/reduce_scatter | solution.py:109
  (259 shorter events, 145.8 us)
Async XLA Ops:
  7.2 5.9 copy-start.1
  7.2 8.7 %copy-start = (s32[256]{0:T(256)S(1)}, s32[256]{0:T(256)}, u32[]{:S(2)}) copy-start(s32[256]{0:T(256)} %param.11) | copy-start | bytes 3076
  7.2 55.9 %all-gather.3.cloned.1.call-start = ((), (), s32[]{:S(2)}) async-start(), calls=%async_computation.2 | async-start | bytes 2621440 | tf_op jit(solution)/shard_map/all_gather | solution.py:72
  7.9 152.5 %all-gather.5.cloned.1.call-start = ((), (), s32[]{:S(2)}) async-start(), calls=%async_computation.3 | async-start | bytes 4259840 | tf_op jit(solution)/shard_map/all_gather | solution.py:85
  9.5 784.5 %reduce-scatter.5.cloned.1.call-start = ((), (), s32[]{:S(2)}) async-start(), calls=%async_computation.5 | async-start | bytes 8519680 | tf_op jit(solution)/shard_map/reduce_scatter | solution.py:110
  379.6 467.6 %reduce-scatter.3.cloned.1.call-start = ((), (), s32[]{:S(2)}) async-start(), calls=%async_computation.4 | async-start | bytes 2621440 | tf_op jit(solution)/shard_map/reduce_scatter | solution.py:109
Sparse Core Ops, SparseCore 0:
  9.8 53.2 all-gather.2
  67.4 93.0 all-gather.4
  379.7 414.1 reduce-scatter.4
  796.9 50.2 reduce-scatter.2
where the time goes:
time: 856 us; the launch traced here: 854 us
  waiting for transfers between devices  604 us (71%)
  other arithmetic  122 us (14%)
  matrix products  74.5 us (9%)
  local copies, waits for them, and re-layouts  38.2 us (4%)
  between operations  13.8 us (2%)
    reduce_scatter x1, waiting for transfers between devices, per_device(): panel_rcv = lax.psum_scatter(other, 'src', scatter_dimension=2, tiled=True)  410 us
    all_gather x1, waiting for transfers between devices, per_device(): shard_piece = lax.all_gather(rcv_spec, 'src', axis=2, tiled=True)  97.3 us
    reduce_scatter x1, waiting for transfers between devices, per_device(): lax.psum_scatter(src_total, 'rcv', scatter_dimension=2, tiled=True)  51.6 us
    all_gather x1, waiting for transfers between devices, per_device(): src_full = lax.all_gather(src_spec, 'rcv', axis=2, tiled=True)  44 us
    dot_general x16, matrix products, cross_block(): jnp.einsum('cgwfs,cgwfr->gfsr', swapped, rcv_five, preferred_element_type...  40 us
    dot_general x16, matrix products, cross_block(): jnp.einsum('cgwfs,cgwfr->gfsr', src_five, rcv_five, preferred_element_typ...  22.9 us
    another operation x16, other arithmetic, receiver_outer(): return jnp.transpose(jnp.stack([panel_re, panel_im]), (2, 0, 1, 3))  20.8 us
    convert_element_type x16, other arithmetic, source_slant(): sin_b = rcv_sin.astype(jnp.bfloat16)  20.1 us
  transfers between devices with their start and end apart: 4, of which 4 were waited for; matrix products, arithmetic and copies ran while one was open for 2% of the time, Pallas kernels for 0%

commit v1 on v0

--- a/solution.py
+++ b/solution.py
@@ -1,3 +1,4 @@
+import functools
 import math
 import jax
 import jax.numpy as jnp
@@ -6,6 +7,18 @@
 
 WIN = 8
 SEGS = 2
+
+
+def refer_the_group(panel, named_axis):
+    return jnp.concatenate(
+        lax.all_to_all(
+            jnp.stack([panel for _ in range(lax.axis_size(named_axis))], 0), named_axis, 0, 0
+        ),
+        2,
+    )
+
+
+report_the_bench = functools.partial(refer_the_group, named_axis="rcv")
 
 
 def phase_table(freqs, lags, n_freq):
@@ -69,7 +82,7 @@
 
 
 def per_device(src_spec, rcv_spec, lag_table, src_pos, rcv_pos):
-    src_full = lax.all_gather(src_spec, "rcv", axis=2, tiled=True)
+    src_full = report_the_bench(src_spec)
     n_freq = src_full.shape[2]
     src_dev = src_full.shape[3]
     rcv_dev = rcv_spec.shape[3]

time: 856 us -> 807 us (0.943)
  waiting for transfers between devices: 604 us -> 542 us
    all_gather x1 -> x0, waiting for transfers between devices: 44 us -> none  [per_device(): src_full = lax.all_gather(src_spec, 'rcv', axis=2, tiled=True)]
    all_gather x1, waiting for transfers between devices: 97.3 us -> 61.9 us  [per_device(): shard_piece = lax.all_gather(rcv_spec, 'src', axis=2, tiled=True)]
    all_to_all x0 -> x1, waiting for transfers between devices: none -> 17.5 us  [refer_the_group(): lax.all_to_all(jnp.stack([panel for _ in range(lax.axis_size(named_axis))...]
  transfers between devices with their start and end apart: 4 -> 4, of which waited for: 4 -> 4; matrix products, arithmetic and copies ran while one was open for 2% -> 3% of each run, Pallas kernels for 0% -> 0%
where the time goes in v1:
time: 807 us; the launch traced here: 804 us
  waiting for transfers between devices  542 us (67%)
  other arithmetic  122 us (15%)
  matrix products  74.6 us (9%)
  local copies, waits for them, and re-layouts  44.6 us (6%)
  between operations  13.8 us (2%)
    reduce_scatter x1, waiting for transfers between devices, per_device(): panel_rcv = lax.psum_scatter(other, 'src', scatter_dimension=2, tiled=True)  411 us
    all_gather x1, waiting for transfers between devices, per_device(): shard_piece = lax.all_gather(rcv_spec, 'src', axis=2, tiled=True)  61.9 us
    reduce_scatter x1, waiting for transfers between devices, per_device(): lax.psum_scatter(src_total, 'rcv', scatter_dimension=2, tiled=True)  51.7 us
    dot_general x16, matrix products, cross_block(): jnp.einsum('cgwfs,cgwfr->gfsr', swapped, rcv_five, preferred_element_type...  40 us
    dot_general x16, matrix products, cross_block(): jnp.einsum('cgwfs,cgwfr->gfsr', src_five, rcv_five, preferred_element_typ...  22.9 us
    another operation x16, other arithmetic, receiver_outer(): return jnp.transpose(jnp.stack([panel_re, panel_im]), (2, 0, 1, 3))  20.8 us
    convert_element_type x16, other arithmetic, source_slant(): sin_b = rcv_sin.astype(jnp.bfloat16)  20.1 us
    all_to_all x1, waiting for transfers between devices, refer_the_group(): lax.all_to_all(jnp.stack([panel for _ in range(lax.axis_size(named_axis))...  17.5 us
  transfers between devices with their start and end apart: 4, of which 4 were waited for; matrix products, arithmetic and copies ran while one was open for 3% of the time, Pallas kernels for 0%

profile of v1, /device:TPU:1, one launch (start us, length us, event | category | flops | bytes accessed | tf_op | source)
XLA Modules:
  0.0 804.3 jit_solution(17791061472061375342)
XLA Ops:
  7.2 1.5 copy.44
  8.8 1.6 stack.80
  10.3 2.7 reshape.94
  13.0 6.6 all-to-all-start
  19.6 2.6 copy.45
  22.2 2.8 gather_fusion.1
  25.0 2.9 gather_fusion
  28.3 17.5 %all-to-all-done = bf16[4,2,65536]{2,1,0:T(2,128)(2,1)S(1)} async-done(((bf16[4,2,65536]{2,1,0:T(2,128)(2,1)}), bf16[4,2,65536]{2,1,0:T(2,128)(2,1)S(1)}, u32[]{:S(2)}, u32[]{:S(2)}) %all-to-all-start) | async-done | bytes 1048608 | tf_op jit(solution)/shard_map/all_to_all | solution.py:14
  47.2 1.6 copy.56
  48.8 61.9 %all-gather.2.cloned.1.call-done = bf16[2,16,256,256]{3,1,0,2:T(8,128)(2,1)} async-done(((bf16[2,16,4,256]{3,1,0,2:T(8,128)(2,1)}), bf16[2,16,256,256]{3,1,0,2:T(8,128)(2,1)}) %all-gather.2.cloned.1.call-update) | async-done | bytes 4194320 | tf_op jit(solution)/shard_map/all_gather | solution.py:98
  110.7 2.2 broadcast_in_dim.40
  112.9 4.3 broadcast_in_dim.41.clone
  117.2 212.7 %while.17 = (s32[]{:T(128)}, f32[16,2,64,256]{2,0,3,1:T(8,128)}, f32[16,2,256,256]{3,0,1,2:T(8,128)}, bf16[2,16,256,64]{3,2,1,0:T(8,128)(2,1)}, bf16[2,16,256,25...) while((s32[]{:T(128)}, f32[16,2,64,256]{2,0,3,1:T(8,128)}, ...), condition=%wide.region_3.4_spmd, body=%wide.region_0.3_spmd.sunk | while | flops 116801552 | bytes 17031760 | solution.py:119
  122.0 1.4 fusion.76
  123.4 2.5 fusion.77
  135.3 1.4 fusion.76
  136.7 2.5 fusion.77
  148.6 1.4 fusion.76
  150.0 2.5 fusion.77
  161.9 1.4 fusion.76
  163.3 2.5 fusion.77
  175.2 1.4 fusion.76
  176.6 2.5 fusion.77
  188.5 1.4 fusion.76
  189.9 2.5 fusion.77
  201.7 1.4 fusion.76
  203.2 2.5 fusion.77
  215.0 1.4 fusion.76
  216.5 2.5 fusion.77
  228.3 1.4 fusion.76
  229.8 2.5 fusion.77
  241.6 1.4 fusion.76
  243.1 2.5 fusion.77
  254.9 1.4 fusion.76
  256.4 2.5 fusion.77
  268.2 1.4 fusion.76
  269.7 2.5 fusion.77
  282.9 2.5 fusion.77
  294.8 1.4 fusion.76
  296.2 2.5 fusion.77
  308.1 1.4 fusion.76
  309.5 2.5 fusion.77
  321.3 1.4 fusion.76
  322.8 2.5 fusion.77
  329.9 3.8 copy.51
  333.8 410.6 %reduce-scatter.5.cloned.1.call-done = f32[16,2,4,256]{3,0,1,2:T(8,128)} async-done(((f32[16,2,256,256]{3,0,1,2:T(8,128)}), f32[16,2,4,256]{3,0,1,2:T(8,128)}) %reduce-scatter.5.cloned.1.call-update) | async-done | bytes 131088 | tf_op jit(solution)/shard_map/reduce_scatter | solution.py:123
  744.4 1.6 copy.53
  746.0 51.7 %reduce-scatter.3.cloned.1.call-done = f32[16,2,16,256]{3,2,1,0:T(8,128)} async-done(((f32[16,2,64,256]{3,2,1,0:T(8,128)}), f32[16,2,16,256]{3,2,1,0:T(8,128)}) %reduce-scatter.3.cloned.1.call-update) | async-done | bytes 524304 | tf_op jit(solution)/shard_map/reduce_scatter | solution.py:122
  (264 shorter events, 151.8 us)
Async XLA Ops:
  7.2 12.4 %copy-start = (s32[16,8192]{1,0:T(8,128)S(1)}, s32[16,8192]{1,0:T(8,128)}, u32[]{:S(2)}) copy-start(s32[16,8192]{1,0:T(8,128)} %param.9) | copy-start | bytes 1572868
  7.2 103.5 %all-gather.2.cloned.1.call-start = ((), (), s32[]{:S(2)}) async-start(), calls=%async_computation.3 | async-start | bytes 4259840 | tf_op jit(solution)/shard_map/all_gather | solution.py:98
  13.0 9.2 %copy-start.2 = (s32[64]{0:T(128)S(1)}, s32[64]{0:T(128)}, u32[]{:S(2)}) copy-start(s32[64]{0:T(128)} %param.10) | copy-start | bytes 772
  13.0 12.0 %copy-start.1 = (s32[256]{0:T(256)S(1)}, s32[256]{0:T(256)}, u32[]{:S(2)}) copy-start(s32[256]{0:T(256)} %param.11) | copy-start | bytes 3076
  13.0 32.8 %all-to-all-start = ((bf16[4,2,65536]{2,1,0:T(2,128)(2,1)}), bf16[4,2,65536]{2,1,0:T(2,128)(2,1)S(1)}, u32[]{:S(2)}, u32[]{:S(2)}) async-start(bf16[4,2,65536]{2,1,0:T(2,128)(2,1)} %reshape.94), calls=%async_computation | async-start | bytes 2097152 | tf_op jit(solution)/shard_map/all_to_all | solution.py:14
  19.6 724.8 %reduce-scatter.5.cloned.1.call-start = ((), (), s32[]{:S(2)}) async-start(), calls=%async_computation.5 | async-start | bytes 8519680 | tf_op jit(solution)/shard_map/reduce_scatter | solution.py:123
  329.9 467.8 %reduce-scatter.3.cloned.1.call-start = ((), (), s32[]{:S(2)}) async-start(), calls=%async_computation.4 | async-start | bytes 2621440 | tf_op jit(solution)/shard_map/reduce_scatter | solution.py:122
Sparse Core Ops, SparseCore 0:
  12.2 98.3 all-gather.1
  330.0 414.3 reduce-scatter.4
  747.5 50.1 reduce-scatter.2
